TPU v7x, 32 devices: a whole 2x2x4 slice. The times are simulated.
32 devices in a mesh: shot: 4 (over z), gx: 4 (over x, core), gy: 2 (over y).
Axes of the slice: x: 2, y: 2, z: 4, core: 2. Of those that a mesh axis runs over, the one named last changes fastest.
Arguments:
- partials: float32 [4, 9, 4, 32, 256], P('shot', None, None, 'gx', 'gy'), may hold values from -16 to 16, as said below
- hist_s: float32 [5, 3, 4, 32, 256], P(None, None, 'shot', 'gx', 'gy'), may hold values from -30 to 30
- hist_y: float32 [5, 3, 4, 32, 256], P(None, None, 'shot', 'gx', 'gy'), may hold values from -70 to 70, as said below
Outputs:
- direction: float32 [3, 4, 32, 256], P(None, 'shot', 'gx', 'gy')
Inputs may be any that keep to these rules, and one draw needn't show every extreme that they name: `partials`: for every shot group and cell, entries 3, 4, 5 are positive and each exceeds the sum of the magnitudes of the two off-diagonal entries of its row of the 3x3 matrix [[e3, e6, e7], [e6, e4, e8], [e7, e8, e5]]. Each entry of hist_y times the matching entry of hist_s is at least 0.2 times the square of that hist_s entry.
All inputs are finite; a program needn't handle non-finite values.
Results may differ from a plain program's by a relative error of at most 0.00013.
Values sent between devices are 32-bit elements; how exact they have to be, the bound alone decides.
No kernel may reach another device: no remote copies, remote signals or barrier semaphores. Data moves between devices by JAX's collectives and lax.ppermute only.
A program may use at most 64 MiB of HBM per device.

v0:
```python
import jax
import jax.numpy as jnp
from jax import lax
from jax.sharding import PartitionSpec as P

PAIRS = 5


def extended_2(cells, sides, width):
    for axis, dim in sides:
        count = lax.axis_size(axis)
        ends = count - 1
        head = lax.slice_in_dim(cells, 0, width, axis=dim)
        tail = lax.slice_in_dim(cells, cells.shape[dim] - width, cells.shape[dim], axis=dim)
        cells = jnp.concatenate(
            [
                lax.ppermute(tail, axis, [(i, (i + 1) % count) for i in range(ends)]),
                cells,
                lax.ppermute(head, axis, [((i + 1) % count, i) for i in range(ends)]),
            ],
            axis=dim,
        )
    return cells


def smooth_block(padded):
    along_x = 0.25 * (padded[:, :, :-2] + 2.0 * padded[:, :, 1:-1] + padded[:, :, 2:])
    return 0.25 * (along_x[..., :-2] + 2.0 * along_x[..., 1:-1] + along_x[..., 2:])


def apply_inverse(hessian, vectors):
    diag_p = hessian[0]
    diag_s = hessian[1]
    diag_r = hessian[2]
    cross_ps = hessian[3]
    cross_pr = hessian[4]
    cross_sr = hessian[5]
    cof_pp = diag_s * diag_r - cross_sr * cross_sr
    cof_ps = cross_pr * cross_sr - cross_ps * diag_r
    cof_pr = cross_ps * cross_sr - diag_s * cross_pr
    cof_ss = diag_p * diag_r - cross_pr * cross_pr
    cof_sr = cross_ps * cross_pr - diag_p * cross_sr
    cof_rr = diag_p * diag_s - cross_ps * cross_ps
    determinant = diag_p * cof_pp + cross_ps * cof_ps + cross_pr * cof_pr
    inverse_det = 1.0 / determinant
    comp_one = vectors[:, 0]
    comp_two = vectors[:, 1]
    comp_three = vectors[:, 2]
    return jnp.stack(
        [
            (cof_pp * comp_one + cof_ps * comp_two + cof_pr * comp_three) * inverse_det,
            (cof_ps * comp_one + cof_ss * comp_two + cof_sr * comp_three) * inverse_det,
            (cof_pr * comp_one + cof_sr * comp_two + cof_rr * comp_three) * inverse_det,
        ],
        axis=1,
    )


def pair_dots(left_flat, right_flat):
    return lax.dot_general(
        left_flat,
        right_flat,
        (((1,), (1,)), ((), ())),
        precision=lax.Precision.HIGHEST,
        preferred_element_type=jnp.float32,
    )


def upper_solve(matrix, values):
    count = matrix.shape[0]
    found = [None] * count
    for row in range(count - 1, -1, -1):
        total = values[row]
        for col in range(row + 1, count):
            total = total - matrix[row, col] * found[col]
        found[row] = total / matrix[row, row]
    return jnp.stack(found)


def upper_transpose_solve(matrix, values):
    count = matrix.shape[0]
    found = [None] * count
    for row in range(count):
        total = values[row]
        for col in range(row):
            total = total - matrix[col, row] * found[col]
        found[row] = total / matrix[row, row]
    return jnp.stack(found)


def combine_terms(cross_gram, curv_gram, hist_dot, pre_dot, solved, hist_s):
    middle_part = jnp.diag(jnp.diag(cross_gram)) + curv_gram
    coef_p = upper_solve(cross_gram, hist_dot)
    right_hand = jnp.dot(middle_part, coef_p, precision=lax.Precision.HIGHEST) - pre_dot
    coef_q = upper_transpose_solve(cross_gram, right_hand)
    update_s = jnp.tensordot(coef_q, hist_s, axes=1, precision=lax.Precision.HIGHEST)
    update_z = jnp.tensordot(coef_p, solved[1:], axes=1, precision=lax.Precision.HIGHEST)
    return -(solved[0] + update_s - update_z)


def per_device(partials, hist_s, hist_y):
    s_flat = hist_s.reshape(PAIRS, -1)
    y_flat = hist_y.reshape(PAIRS, -1)
    inverse_count = 1.0 / lax.axis_size("shot")
    level_sums = lax.psum_scatter(partials[0], "shot", scatter_dimension=1, tiled=True)
    fields = level_sums * inverse_count
    extended = extended_2(fields, (("gx", 2), ("gy", 3)), 1)
    smoothed = smooth_block(extended)
    gradient = smoothed[0:3]
    solved = apply_inverse(smoothed[3:9], jnp.concatenate([gradient[None], hist_y], axis=0))
    z_flat = solved[1:].reshape(PAIRS, -1)
    curv_part = pair_dots(y_flat, z_flat)
    hist_part = pair_dots(s_flat, gradient.reshape(1, -1))[:, 0]
    pre_part = pair_dots(y_flat, solved[0].reshape(1, -1))[:, 0]
    cross_gram, curv_gram, hist_dot, pre_dot = lax.psum(
        (pair_dots(s_flat, y_flat), curv_part, hist_part, pre_part), ("shot", "gx", "gy")
    )
    return combine_terms(cross_gram, curv_gram, hist_dot, pre_dot, solved, hist_s)


def solution(mesh):
    return jax.shard_map(
        per_device,
        mesh=mesh,
        in_specs=(
            P("shot", None, None, "gx", "gy"),
            P(None, None, "shot", "gx", "gy"),
            P(None, None, "shot", "gx", "gy"),
        ),
        out_specs=P(None, "shot", "gx", "gy"),
        check_vma=False,
    )
```

profile of v0, /device:TPU:14, one launch (start us, length us, event | category | flops | bytes accessed | tf_op | source)
XLA Modules:
  0.0 124.9 jit_solution(4067416101223130220)
XLA Ops:
  6.5 0.0 reduce-scatter.4.cloned.1.call-start
  6.5 1.6 %copy.40 = f32[1,9,4,8,128]{4,3,1,2,0:T(8,128)} copy(f32[1,9,4,8,128]{4,3,2,1,0:T(8,128)} %param.3) | data formatting | bytes 294912 | tf_op args[0]
  8.1 0.0 reduce-scatter.4.cloned.1.call-update
  8.1 19.2 %reduce-scatter.4.cloned.1.call-done = f32[9,1,8,128]{3,2,0,1:T(8,128)} async-done(((f32[9,4,8,128]{3,2,0,1:T(8,128)}), f32[9,1,8,128]{3,2,0,1:T(8,128)}) %reduce-scatter.4.cloned.1.call-update) | async-done | bytes 36880
  27.4 0.8 broadcast_multiply_fusion
  28.2 1.9 %collective-permute-start = (f32[9,1,1,128]{3,2,0,1:T(1,128)S(1)}, f32[9,1,1,128]{3,2,0,1:T(1,128)S(1)}, u32[]{:S(2)}, u32[]{:S(2)}) collective-permute-start(f32[9,1,1,128]{3,2,0,1:T(1,128)S(1)} %get-tuple-element.25), channel_id=1, source_target_pairs={{0,2},{2,4},{4,6},{1,3},{3,5},{5,7},{8,10},{10,12},{12,14},{9,11},... | collective-permute-start | bytes 13832 | tf_op jit(solution)/shard_map/ppermute | solution.py:17
  30.1 3.6 %collective-permute-start.1 = (f32[9,1,1,128]{3,2,0,1:T(1,128)S(1)}, f32[9,1,1,128]{3,2,0,1:T(1,128)S(1)}, u32[]{:S(2)}, u32[]{:S(2)}) collective-permute-start(f32[9,1,1,128]{3,2,0,1:T(1,128)S(1)} %get-tuple-element.26), channel_id=1, source_target_pairs={{2,0},{4,2},{6,4},{3,1},{5,3},{7,5},{10,8},{12,10},{14,12},{11,9},... | collective-permute-start | bytes 13832 | tf_op jit(solution)/shard_map/ppermute | solution.py:19
  33.7 0.0 collective-permute-done
  33.8 1.3 %collective-permute-done.1 = f32[9,1,1,128]{3,2,0,1:T(1,128)S(1)} collective-permute-done((f32[9,1,1,128]{3,2,0,1:T(1,128)S(1)}, f32[9,1,1,128]{3,2,0,1:T(1,128)S(1)}, u32[]{:S(2)}, u32[]{:S(2)}) %collective-permute-start.1) | collective-permute-done | bytes 4640 | tf_op jit(solution)/shard_map/ppermute | solution.py:19
  35.1 0.0 copy-start
  35.1 0.0 copy-start.1
  35.1 0.1 fusion.26
  35.2 1.3 %collective-permute-start.2 = (f32[9,1,10,1]{3,2,0,1:T(8,128)S(1)}, f32[9,1,10,1]{3,2,0,1:T(8,128)S(1)}, u32[]{:S(2)}, u32[]{:S(2)}) collective-permute-start(f32[9,1,10,1]{3,2,0,1:T(8,128)S(1)} %get-tuple-element.16), channel_id=1, source_target_pairs={{0,1},{2,3},{4,5},{6,7},{8,9},{10,11},{12,13},{14,15},{16,17},{18,... | collective-permute-start | bytes 1088 | tf_op jit(solution)/shard_map/ppermute | solution.py:17
  36.5 4.5 %collective-permute-start.3 = (f32[9,1,10,1]{3,2,0,1:T(8,128)S(1)}, f32[9,1,10,1]{3,2,0,1:T(8,128)S(1)}, u32[]{:S(2)}, u32[]{:S(2)}) collective-permute-start(f32[9,1,10,1]{3,2,0,1:T(8,128)S(1)} %get-tuple-element.17), channel_id=1, source_target_pairs={{1,0},{3,2},{5,4},{7,6},{9,8},{11,10},{13,12},{15,14},{17,16},{19,... | collective-permute-start | bytes 1088 | tf_op jit(solution)/shard_map/ppermute | solution.py:19
  41.0 0.0 copy-done
  41.0 0.0 copy-done.1
  41.1 0.3 convolution_bitcast_fusion.1
  41.3 0.1 copy.13
  41.4 0.0 collective-permute-done.2
  41.4 1.6 %collective-permute-done.3 = f32[9,1,10,1]{3,2,0,1:T(8,128)S(1)} collective-permute-done((f32[9,1,10,1]{3,2,0,1:T(8,128)S(1)}, f32[9,1,10,1]{3,2,0,1:T(8,128)S(1)}, u32[]{:S(2)}, u32[]{:S(2)}) %collective-permute-start.3) | collective-permute-done | bytes 392 | tf_op jit(solution)/shard_map/ppermute | solution.py:19
  43.0 0.2 pad_maximum_fusion
  43.2 0.1 fusion.12
  43.4 0.3 convolution_bitcast_fusion
  43.7 0.1 pad_maximum_fusion.5
  43.8 0.3 convolution_bitcast_fusion.4
  44.0 0.3 convolution_bitcast_fusion.3
  44.4 0.1 or_bitcast_fusion
  44.4 43.8 %all-reduce.1 = (f32[5]{0:T(128)S(1)}, f32[5,5]{1,0:T(8,128)S(1)}, f32[5]{0:T(128)S(1)}, f32[5,5]{0,1:T(8,128)S(1)}) all-reduce(f32[5]{0:T(128)S(1)} %convolution_bitcast_fusion.4, f32[5,5]{1,0:T(8,128)S(1)} %convolution_bitcast_fusion.1, ...), channel_id=1, replica_groups=mesh['shot'=4,'gx'=4,'gy'=2] {'shot','gx','gy'}, use_global_device_ids=true, to_apply=%region_3.0 | all-reduce | flops 60 | bytes 480 | tf_op jit(solution)/shard_map/psum | solution.py:115
  88.3 0.7 fusion.28
  89.0 0.7 fusion.30
  99.2 0.6 gather_fusion
  103.1 0.1 stack.48
  103.2 0.1 fusion
  103.3 0.7 fusion.29
  116.9 0.1 stack.54
  116.9 0.2 fusion.1
  117.2 0.2 fusion.21
  117.4 0.6 negate_bitcast_fusion
  (8 shorter events, 0.2 us)
Async XLA Ops:
  6.5 20.8 %reduce-scatter.4.cloned.1.call-start = ((), (), s32[]{:S(2)}) async-start(), calls=%async_computation.1 | async-start | bytes 184320
  28.2 5.6 %collective-permute-start = (f32[9,1,1,128]{3,2,0,1:T(1,128)S(1)}, f32[9,1,1,128]{3,2,0,1:T(1,128)S(1)}, u32[]{:S(2)}, u32[]{:S(2)}) collective-permute-start(f32[9,1,1,128]{3,2,0,1:T(1,128)S(1)} %get-tuple-element.25), channel_id=1, source_target_pairs={{0,2},{2,4},{4,6},{1,3},{3,5},{5,7},{8,10},{10,12},{12,14},{9,11},... | collective-permute-start | bytes 13832 | tf_op jit(solution)/shard_map/ppermute | solution.py:17
  30.1 5.0 %collective-permute-start.1 = (f32[9,1,1,128]{3,2,0,1:T(1,128)S(1)}, f32[9,1,1,128]{3,2,0,1:T(1,128)S(1)}, u32[]{:S(2)}, u32[]{:S(2)}) collective-permute-start(f32[9,1,1,128]{3,2,0,1:T(1,128)S(1)} %get-tuple-element.26), channel_id=1, source_target_pairs={{2,0},{4,2},{6,4},{3,1},{5,3},{7,5},{10,8},{12,10},{14,12},{11,9},... | collective-permute-start | bytes 13832 | tf_op jit(solution)/shard_map/ppermute | solution.py:19
  35.1 6.0 %copy-start = (f32[5,3,1,8,128]{4,3,2,1,0:T(8,128)S(1)}, f32[5,3,1,8,128]{4,3,2,1,0:T(8,128)}, u32[]{:S(2)}) copy-start(f32[5,3,1,8,128]{4,3,2,1,0:T(8,128)} %param.5) | copy-start | bytes 184324
  35.1 6.0 %copy-start.1 = (f32[5,3,1,8,128]{4,3,2,1,0:T(8,128)S(1)}, f32[5,3,1,8,128]{4,3,2,1,0:T(8,128)}, u32[]{:S(2)}) copy-start(f32[5,3,1,8,128]{4,3,2,1,0:T(8,128)} %param.4) | copy-start | bytes 184324
  35.2 6.2 %collective-permute-start.2 = (f32[9,1,10,1]{3,2,0,1:T(8,128)S(1)}, f32[9,1,10,1]{3,2,0,1:T(8,128)S(1)}, u32[]{:S(2)}, u32[]{:S(2)}) collective-permute-start(f32[9,1,10,1]{3,2,0,1:T(8,128)S(1)} %get-tuple-element.16), channel_id=1, source_target_pairs={{0,1},{2,3},{4,5},{6,7},{8,9},{10,11},{12,13},{14,15},{16,17},{18,... | collective-permute-start | bytes 1088 | tf_op jit(solution)/shard_map/ppermute | solution.py:17
  36.5 6.5 %collective-permute-start.3 = (f32[9,1,10,1]{3,2,0,1:T(8,128)S(1)}, f32[9,1,10,1]{3,2,0,1:T(8,128)S(1)}, u32[]{:S(2)}, u32[]{:S(2)}) collective-permute-start(f32[9,1,10,1]{3,2,0,1:T(8,128)S(1)} %get-tuple-element.17), channel_id=1, source_target_pairs={{1,0},{3,2},{5,4},{7,6},{9,8},{11,10},{13,12},{15,14},{17,16},{19,... | collective-permute-start | bytes 1088 | tf_op jit(solution)/shard_map/ppermute | solution.py:19
Sparse Core Ops, SparseCore 0:
  9.6 17.7 reduce-scatter.3
where the time goes:
time: 126 us; the launch traced here: 125 us
  blocking collectives  43.8 us (35%)
  between operations  39.2 us (31%)
  waiting for transfers between devices  22.1 us (18%)
  starting transfers between devices  11.4 us (9%)
  local copies, waits for them, and re-layouts  4.65 us (4%)
  other arithmetic  1.9 us (2%)
  matrix products  1.73 us (1%)
    psum x1, blocking collectives, per_device(): lax.psum((pair_dots(s_flat, y_flat), curv_part, hist_part, pre_part), ('s...  43.8 us
    unnamed x2, waiting for transfers between devices  19.3 us
    ppermute x2, starting transfers between devices, extended_2(): lax.ppermute(head, axis, [((i + 1) % count, i) for i in range(ends)])  8.19 us
    ppermute x2, starting transfers between devices, extended_2(): lax.ppermute(tail, axis, [(i, (i + 1) % count) for i in range(ends)])  3.21 us
    ppermute x2, waiting for transfers between devices, extended_2(): lax.ppermute(head, axis, [((i + 1) % count, i) for i in range(ends)])  2.87 us
  transfers between devices with their start and end apart: 5, of which 3 were waited for; matrix products, arithmetic and copies ran while one was open for 0% of the time, Pallas kernels for 0%

commit v1 on v0

--- a/solution.py
+++ b/solution.py
@@ -113,7 +113,7 @@
     hist_part = pair_dots(s_flat, gradient.reshape(1, -1))[:, 0]
     pre_part = pair_dots(y_flat, solved[0].reshape(1, -1))[:, 0]
     cross_gram, curv_gram, hist_dot, pre_dot = lax.psum(
-        (pair_dots(s_flat, y_flat), curv_part, hist_part, pre_part), ("shot", "gx", "gy")
+        lax.psum((pair_dots(s_flat, y_flat), curv_part, hist_part, pre_part), ("gx", "gy")), "shot"
     )
     return combine_terms(cross_gram, curv_gram, hist_dot, pre_dot, solved, hist_s)
 

time: 126 us -> 109 us (0.87)
  blocking collectives: 43.8 us -> 27.2 us
    psum x1 -> x2, blocking collectives: 43.8 us -> 27.2 us  [the longest x1 15.2 us: per_device(): lax.psum((pair_dots(s_flat, y_flat), curv_part, hist_part, pre_part), ('g...]
where the time goes in v1:
time: 109 us; the launch traced here: 108 us
  between operations  39.1 us (36%)
  blocking collectives  27.2 us (25%)
  waiting for transfers between devices  22.2 us (20%)
  starting transfers between devices  11.4 us (10%)
  local copies, waits for them, and re-layouts  4.64 us (4%)
  other arithmetic  1.9 us (2%)
  matrix products  1.72 us (2%)
    unnamed x2, waiting for transfers between devices  19.3 us
    psum x1, blocking collectives, per_device(): lax.psum((pair_dots(s_flat, y_flat), curv_part, hist_part, pre_part), ('g...  15.2 us
    psum x1, blocking collectives, per_device(): lax.psum(lax.psum((pair_dots(s_flat, y_flat), curv_part, hist_part, pre_p...  11.9 us
    ppermute x2, starting transfers between devices, extended_2(): lax.ppermute(head, axis, [((i + 1) % count, i) for i in range(ends)])  8.19 us
    ppermute x2, starting transfers between devices, extended_2(): lax.ppermute(tail, axis, [(i, (i + 1) % count) for i in range(ends)])  3.21 us
    ppermute x2, waiting for transfers between devices, extended_2(): lax.ppermute(head, axis, [((i + 1) % count, i) for i in range(ends)])  2.87 us
  transfers between devices with their start and end apart: 5, of which 3 were waited for; matrix products, arithmetic and copies ran while one was open for 0% of the time, Pallas kernels for 0%

profile of v1, /device:TPU:14, one launch (start us, length us, event | category | flops | bytes accessed | tf_op | source)
XLA Modules:
  0.0 108.1 jit_solution(15997432623930500243)
XLA Ops:
  6.5 0.0 reduce-scatter.4.cloned.1.call-start
  6.5 1.6 %copy.40 = f32[1,9,4,8,128]{4,3,1,2,0:T(8,128)} copy(f32[1,9,4,8,128]{4,3,2,1,0:T(8,128)} %param.3) | data formatting | bytes 294912 | tf_op args[0]
  8.1 0.0 reduce-scatter.4.cloned.1.call-update
  8.1 19.2 %reduce-scatter.4.cloned.1.call-done = f32[9,1,8,128]{3,2,0,1:T(8,128)} async-done(((f32[9,4,8,128]{3,2,0,1:T(8,128)}), f32[9,1,8,128]{3,2,0,1:T(8,128)}) %reduce-scatter.4.cloned.1.call-update) | async-done | bytes 36880
  27.4 0.8 broadcast_multiply_fusion
  28.2 1.9 %collective-permute-start = (f32[9,1,1,128]{3,2,0,1:T(1,128)S(1)}, f32[9,1,1,128]{3,2,0,1:T(1,128)S(1)}, u32[]{:S(2)}, u32[]{:S(2)}) collective-permute-start(f32[9,1,1,128]{3,2,0,1:T(1,128)S(1)} %get-tuple-element.29), channel_id=1, source_target_pairs={{0,2},{2,4},{4,6},{1,3},{3,5},{5,7},{8,10},{10,12},{12,14},{9,11},... | collective-permute-start | bytes 13832 | tf_op jit(solution)/shard_map/ppermute | solution.py:17
  30.1 3.6 %collective-permute-start.1 = (f32[9,1,1,128]{3,2,0,1:T(1,128)S(1)}, f32[9,1,1,128]{3,2,0,1:T(1,128)S(1)}, u32[]{:S(2)}, u32[]{:S(2)}) collective-permute-start(f32[9,1,1,128]{3,2,0,1:T(1,128)S(1)} %get-tuple-element.30), channel_id=1, source_target_pairs={{2,0},{4,2},{6,4},{3,1},{5,3},{7,5},{10,8},{12,10},{14,12},{11,9},... | collective-permute-start | bytes 13832 | tf_op jit(solution)/shard_map/ppermute | solution.py:19
  33.7 0.0 collective-permute-done
  33.8 1.3 %collective-permute-done.1 = f32[9,1,1,128]{3,2,0,1:T(1,128)S(1)} collective-permute-done((f32[9,1,1,128]{3,2,0,1:T(1,128)S(1)}, f32[9,1,1,128]{3,2,0,1:T(1,128)S(1)}, u32[]{:S(2)}, u32[]{:S(2)}) %collective-permute-start.1) | collective-permute-done | bytes 4640 | tf_op jit(solution)/shard_map/ppermute | solution.py:19
  35.1 0.0 copy-start
  35.1 0.0 copy-start.1
  35.1 0.1 fusion.26
  35.2 1.3 %collective-permute-start.2 = (f32[9,1,10,1]{3,2,0,1:T(8,128)S(1)}, f32[9,1,10,1]{3,2,0,1:T(8,128)S(1)}, u32[]{:S(2)}, u32[]{:S(2)}) collective-permute-start(f32[9,1,10,1]{3,2,0,1:T(8,128)S(1)} %get-tuple-element.20), channel_id=1, source_target_pairs={{0,1},{2,3},{4,5},{6,7},{8,9},{10,11},{12,13},{14,15},{16,17},{18,... | collective-permute-start | bytes 1088 | tf_op jit(solution)/shard_map/ppermute | solution.py:17
  36.5 4.5 %collective-permute-start.3 = (f32[9,1,10,1]{3,2,0,1:T(8,128)S(1)}, f32[9,1,10,1]{3,2,0,1:T(8,128)S(1)}, u32[]{:S(2)}, u32[]{:S(2)}) collective-permute-start(f32[9,1,10,1]{3,2,0,1:T(8,128)S(1)} %get-tuple-element.21), channel_id=1, source_target_pairs={{1,0},{3,2},{5,4},{7,6},{9,8},{11,10},{13,12},{15,14},{17,16},{19,... | collective-permute-start | bytes 1088 | tf_op jit(solution)/shard_map/ppermute | solution.py:19
  41.0 0.0 copy-done
  41.0 0.0 copy-done.1
  41.1 0.3 convolution_bitcast_fusion.1
  41.3 0.1 copy.13
  41.4 0.0 collective-permute-done.2
  41.4 1.6 %collective-permute-done.3 = f32[9,1,10,1]{3,2,0,1:T(8,128)S(1)} collective-permute-done((f32[9,1,10,1]{3,2,0,1:T(8,128)S(1)}, f32[9,1,10,1]{3,2,0,1:T(8,128)S(1)}, u32[]{:S(2)}, u32[]{:S(2)}) %collective-permute-start.3) | collective-permute-done | bytes 392 | tf_op jit(solution)/shard_map/ppermute | solution.py:19
  43.0 0.2 pad_maximum_fusion
  43.2 0.1 fusion.12
  43.4 0.3 convolution_bitcast_fusion
  43.7 0.1 pad_maximum_fusion.5
  43.8 0.3 convolution_bitcast_fusion.4
  44.0 0.3 convolution_bitcast_fusion.3
  44.4 0.1 or_bitcast_fusion
  44.4 15.2 %all-reduce.1 = (f32[5]{0:T(128)S(1)}, f32[5,5]{1,0:T(8,128)S(1)}, f32[5]{0:T(128)S(1)}, f32[5,5]{0,1:T(8,128)S(1)}) all-reduce(f32[5]{0:T(128)S(1)} %convolution_bitcast_fusion.4, f32[5,5]{1,0:T(8,128)S(1)} %convolution_bitcast_fusion.1, f32[5]{0:T(128)S(1)} %convolution_bitcast_fusion.3, ...), channel_id=1, replica_groups=mesh['shot'=4,'gx'=4,'gy'=2] {'gx','gy'}, use_global_device_ids=true, to_apply=%region_5.0 | all-reduce | flops 60 | bytes 480 | tf_op jit(solution)/shard_map/psum | solution.py:116
  59.7 11.9 %all-reduce.2 = (f32[5]{0:T(128)S(1)}, f32[5,5]{1,0:T(8,128)S(1)}, f32[5]{0:T(128)S(1)}, f32[5,5]{0,1:T(8,128)S(1)}) all-reduce(f32[5]{0:T(128)S(1)} %get-tuple-element.5, f32[5,5]{1,0:T(8,128)S(1)} %get-tuple-element.6, f32[5]{0:T(128)S(1)} %get-tuple-element.7, ...), channel_id=1, replica_groups=mesh['shot'=4,'gx'=4,'gy'=2] {'shot'}, use_global_device_ids=true, to_apply=%region_6.0 | all-reduce | flops 60 | bytes 480 | tf_op jit(solution)/shard_map/psum | solution.py:115
  71.6 0.7 fusion.28
  72.3 0.7 fusion.30
  82.4 0.6 gather_fusion
  86.4 0.1 stack.48
  86.5 0.1 fusion
  86.7 0.7 fusion.29
  100.1 0.1 stack.54
  100.2 0.2 fusion.1
  100.4 0.2 fusion.21
  100.7 0.6 negate_bitcast_fusion
  (8 shorter events, 0.2 us)
Async XLA Ops:
  6.5 20.8 %reduce-scatter.4.cloned.1.call-start = ((), (), s32[]{:S(2)}) async-start(), calls=%async_computation.1 | async-start | bytes 184320
  28.2 5.6 %collective-permute-start = (f32[9,1,1,128]{3,2,0,1:T(1,128)S(1)}, f32[9,1,1,128]{3,2,0,1:T(1,128)S(1)}, u32[]{:S(2)}, u32[]{:S(2)}) collective-permute-start(f32[9,1,1,128]{3,2,0,1:T(1,128)S(1)} %get-tuple-element.29), channel_id=1, source_target_pairs={{0,2},{2,4},{4,6},{1,3},{3,5},{5,7},{8,10},{10,12},{12,14},{9,11},... | collective-permute-start | bytes 13832 | tf_op jit(solution)/shard_map/ppermute | solution.py:17
  30.1 5.0 %collective-permute-start.1 = (f32[9,1,1,128]{3,2,0,1:T(1,128)S(1)}, f32[9,1,1,128]{3,2,0,1:T(1,128)S(1)}, u32[]{:S(2)}, u32[]{:S(2)}) collective-permute-start(f32[9,1,1,128]{3,2,0,1:T(1,128)S(1)} %get-tuple-element.30), channel_id=1, source_target_pairs={{2,0},{4,2},{6,4},{3,1},{5,3},{7,5},{10,8},{12,10},{14,12},{11,9},... | collective-permute-start | bytes 13832 | tf_op jit(solution)/shard_map/ppermute | solution.py:19
  35.1 6.0 %copy-start = (f32[5,3,1,8,128]{4,3,2,1,0:T(8,128)S(1)}, f32[5,3,1,8,128]{4,3,2,1,0:T(8,128)}, u32[]{:S(2)}) copy-start(f32[5,3,1,8,128]{4,3,2,1,0:T(8,128)} %param.5) | copy-start | bytes 184324
  35.1 6.0 %copy-start.1 = (f32[5,3,1,8,128]{4,3,2,1,0:T(8,128)S(1)}, f32[5,3,1,8,128]{4,3,2,1,0:T(8,128)}, u32[]{:S(2)}) copy-start(f32[5,3,1,8,128]{4,3,2,1,0:T(8,128)} %param.4) | copy-start | bytes 184324
  35.2 6.2 %collective-permute-start.2 = (f32[9,1,10,1]{3,2,0,1:T(8,128)S(1)}, f32[9,1,10,1]{3,2,0,1:T(8,128)S(1)}, u32[]{:S(2)}, u32[]{:S(2)}) collective-permute-start(f32[9,1,10,1]{3,2,0,1:T(8,128)S(1)} %get-tuple-element.20), channel_id=1, source_target_pairs={{0,1},{2,3},{4,5},{6,7},{8,9},{10,11},{12,13},{14,15},{16,17},{18,... | collective-permute-start | bytes 1088 | tf_op jit(solution)/shard_map/ppermute | solution.py:17
  36.5 6.5 %collective-permute-start.3 = (f32[9,1,10,1]{3,2,0,1:T(8,128)S(1)}, f32[9,1,10,1]{3,2,0,1:T(8,128)S(1)}, u32[]{:S(2)}, u32[]{:S(2)}) collective-permute-start(f32[9,1,10,1]{3,2,0,1:T(8,128)S(1)} %get-tuple-element.21), channel_id=1, source_target_pairs={{1,0},{3,2},{5,4},{7,6},{9,8},{11,10},{13,12},{15,14},{17,16},{19,... | collective-permute-start | bytes 1088 | tf_op jit(solution)/shard_map/ppermute | solution.py:19
Sparse Core Ops, SparseCore 0:
  9.6 17.7 reduce-scatter.3
